TPU v7x, 32 devices: a whole 2x2x4 slice. The times are simulated.
32 devices in a mesh: dp: 2 (over x), wide: 4 (over z), narrow: 4 (over y, core).
Axes of the slice: x: 2, y: 2, z: 4, core: 2. Of those that a mesh axis runs over, the one named last changes fastest.
Arguments:
- tokens: bfloat16 [8192, 2048], P(('dp', 'wide'), 'narrow'), may hold values from -6 to 6
- continuation_lengths: int32 [2, 8], P('dp'), may hold values from 1 to 511, 2048 in all within a row
- attention_gain: float32 [2048], replicated, may hold values from 0.5 to 1.5
- query_weight: bfloat16 [2048, 2048], P('narrow', 'wide'), may hold values from -0.125 to 0.125
- key_weight: bfloat16 [2048, 1024], P('narrow', 'wide'), may hold values from -0.125 to 0.125
- value_weight: bfloat16 [2048, 1024], P('narrow', 'wide'), may hold values from -0.125 to 0.125
- head_gate: bfloat16 [2048, 16], P('narrow', 'wide'), may hold values from -0.125 to 0.125
- query_gain: float32 [128], replicated, may hold values from 0.5 to 1.5
- key_gain: float32 [128], replicated, may hold values from 0.5 to 1.5
- output_weight: bfloat16 [2048, 2048], P('wide', 'narrow'), may hold values from -2 to 2
- feedforward_gain: float32 [2048], replicated, may hold values from 0.5 to 1.5
- gate_weight: bfloat16 [2048, 6144], P('narrow', 'wide'), may hold values from -0.125 to 0.125
- up_weight: bfloat16 [2048, 6144], P('narrow', 'wide'), may hold values from -0.125 to 0.125
- down_weight: bfloat16 [6144, 2048], P('wide', 'narrow'), may hold values from -0.078125 to 0.078125
- cotangent: bfloat16 [8192, 2048], P(('dp', 'wide'), 'narrow'), may hold values from -6 to 6
Outputs:
- layer_output: bfloat16 [8192, 2048], P(('dp', 'wide'), 'narrow')
- tokens_gradient: float32 [8192, 2048], P(('dp', 'wide'), 'narrow')
- attention_gain_gradient: float32 [2048], replicated
- query_gradient: float32 [2048, 2048], P('narrow', 'wide')
- key_gradient: float32 [2048, 1024], P('narrow', 'wide')
- value_gradient: float32 [2048, 1024], P('narrow', 'wide')
- head_gate_gradient: float32 [2048, 16], P('narrow', 'wide')
- query_gain_gradient: float32 [128], replicated
- key_gain_gradient: float32 [128], replicated
- output_gradient: float32 [2048, 2048], P('wide', 'narrow')
- feedforward_gain_gradient: float32 [2048], replicated
- gate_gradient: float32 [2048, 6144], P('narrow', 'wide')
- up_gradient: float32 [2048, 6144], P('narrow', 'wide')
- down_gradient: float32 [6144, 2048], P('wide', 'narrow')
Inputs may be any that keep to these rules, and one draw needn't show every extreme that they name: `continuation_lengths`: each group's 8 lengths sum to 2048, and one of them is exactly 511.
All inputs are finite; a program needn't handle non-finite values.
Results may differ from a plain program's by a relative error of at most 0.018.
Values may be sent and summed in bfloat16 or wider, within the bound.
A program may use at most 320 MiB of HBM per device.

v0:
```python
import jax
import jax.numpy as jnp
from jax import lax
from jax.sharding import PartitionSpec as P

PROMPT = 2048
EPS = 1e-06
THETA = 1000000.0


def dot_rows(left, right):
    return jnp.dot(left, right, preferred_element_type=jnp.float32)


def dot_trans(left, right):
    return lax.dot_general(
        left, right, (((1,), (1,)), ((), ())), preferred_element_type=jnp.float32
    )


def dot_inner(left, right):
    return lax.dot_general(
        left, right, (((0,), (0,)), ((), ())), preferred_element_type=jnp.float32
    )


def expand(local_rows, weight, transpose):
    gathered = lax.all_gather(local_rows, "wide", axis=0, tiled=True)

    def expand_partial_term():
        if transpose:
            return dot_trans(gathered, weight)
        return dot_rows(gathered, weight)

    return (
        gathered,
        lax.psum_scatter(expand_partial_term(), "narrow", scatter_dimension=0, tiled=True),
    )


def contract(local_rows, weight, transpose):
    gathered = lax.all_gather(local_rows, "narrow", axis=0, tiled=True)

    def contract_partial_term():
        if transpose:
            return dot_trans(gathered, weight)
        return dot_rows(gathered, weight)

    return (
        gathered,
        lax.psum_scatter(contract_partial_term(), "wide", scatter_dimension=0, tiled=True),
    )


def row_total(values):
    return lax.psum(values, "narrow")


def layout(lengths, group_rows):
    ends = jnp.cumsum(lengths)
    starts = ends - lengths
    index = jnp.arange(group_rows, dtype=jnp.int32)
    offset = index - PROMPT
    member = ((offset[:, None] >= starts[None, :]) & (offset[:, None] < ends[None, :])).astype(
        jnp.int32
    )
    numbers = jnp.arange(1, lengths.shape[0] + 1, dtype=jnp.int32)
    segment = jnp.sum(member * numbers[None, :], axis=1)
    position = index - jnp.sum(member * starts[None, :], axis=1)
    return (index, segment, position)


def rope_tables(position, head_size):
    frequency = THETA ** (-2.0 * jnp.arange(head_size // 2, dtype=jnp.float32) / head_size)
    angle = position.astype(jnp.float32)[:, None] * frequency[None, :]
    return (jnp.cos(angle)[:, None, :], jnp.sin(angle)[:, None, :])


def rotate(values, cosine, sine):
    half = values.shape[-1] // 2
    first = values[..., :half]
    second = values[..., half:]
    return jnp.concatenate(
        [first * cosine - second * sine, second * cosine + first * sine], axis=-1
    )


def rotate_back(upstream, cosine, sine):
    half = upstream.shape[-1] // 2
    first = upstream[..., :half]
    second = upstream[..., half:]
    return jnp.concatenate(
        [first * cosine + second * sine, second * cosine - first * sine], axis=-1
    )


def head_norm(raw, gain):
    inverse = lax.rsqrt(jnp.mean(raw * raw, axis=-1, keepdims=True) + EPS)
    normal = raw * inverse
    return (normal, inverse, normal * gain)


def head_norm_back(upstream, normal, inverse, gain):
    scaled = upstream * gain
    gain_term = jnp.sum(upstream * normal, axis=(0, 1))
    inner = jnp.mean(scaled * normal, axis=-1, keepdims=True)
    return (inverse * (scaled - normal * inner), gain_term)


def visible(row_index, row_segment, index, segment):
    return (index[None, :] <= row_index[:, None]) & (
        (segment[None, :] == 0) | (segment[None, :] == row_segment[:, None])
    )


def block_scores(grouped, keys_all, allowed, scale):
    scores = (
        jnp.einsum("bkrd,tkd->krbt", grouped, keys_all, preferred_element_type=jnp.float32) * scale
    )
    return jnp.where(allowed[None, None], scores, -1e30)


def on_device(
    tokens,
    continuation_lengths,
    attention_gain,
    query_weight,
    key_weight,
    value_weight,
    head_gate,
    query_gain,
    key_gain,
    output_weight,
    feedforward_gain,
    gate_weight,
    up_weight,
    down_weight,
    cotangent,
):
    rows_wide, width_local = tokens.shape
    width_full = attention_gain.shape[0]
    head_size = query_gain.shape[0]
    heads_local = head_gate.shape[1]
    pair_heads = key_weight.shape[1] // head_size
    hidden_local = gate_weight.shape[1]
    group_rows = rows_wide * lax.axis_size("wide")
    rows_narrow = group_rows // lax.axis_size("narrow")
    narrow_index = lax.axis_index("narrow")
    repeat = heads_local // pair_heads
    block = 512
    blocks = rows_narrow // block
    scale = head_size ** (-0.5)
    query_cols = heads_local * head_size
    key_cols = pair_heads * head_size
    index, segment, position = layout(continuation_lengths[0], group_rows)
    my_start = narrow_index * rows_narrow
    my_index = lax.dynamic_slice_in_dim(index, my_start, rows_narrow)
    my_segment = lax.dynamic_slice_in_dim(segment, my_start, rows_narrow)
    my_position = lax.dynamic_slice_in_dim(position, my_start, rows_narrow)
    cosine, sine = rope_tables(my_position, head_size)
    gain_one = lax.dynamic_slice_in_dim(attention_gain, narrow_index * width_local, width_local)
    gain_two = lax.dynamic_slice_in_dim(feedforward_gain, narrow_index * width_local, width_local)
    inputs = tokens.astype(jnp.float32)
    inverse_one = lax.rsqrt(row_total(jnp.sum(inputs * inputs, axis=1)) / width_full + EPS)[:, None]
    hat_one = inputs * inverse_one
    normed = (hat_one * gain_one).astype(jnp.bfloat16)
    joined_weight = jnp.concatenate([query_weight, key_weight, value_weight, head_gate], axis=1)
    normed_all, projected = expand(normed, joined_weight, False)
    query_raw = projected[:, :query_cols].reshape(rows_narrow, heads_local, head_size)
    key_raw = projected[:, query_cols : query_cols + key_cols].reshape(
        rows_narrow, pair_heads, head_size
    )
    value_raw = projected[:, query_cols + key_cols : query_cols + 2 * key_cols]
    gate_logit = projected[:, query_cols + 2 * key_cols :]
    query_hat, query_inverse, query_normed = head_norm(query_raw, query_gain)
    key_hat, key_inverse, key_normed = head_norm(key_raw, key_gain)
    queries = rotate(query_normed, cosine, sine).astype(jnp.bfloat16)
    keys_local = rotate(key_normed, cosine, sine).astype(jnp.bfloat16)
    values_local = value_raw.reshape(rows_narrow, pair_heads, head_size).astype(jnp.bfloat16)
    keys_all, values_all = (
        lax.all_gather(keys_local, "narrow", axis=0, tiled=True),
        lax.all_gather(values_local, "narrow", axis=0, tiled=True),
    )

    def attend(block_inputs):
        query_block, row_index, row_segment = block_inputs
        grouped = query_block.reshape(block, pair_heads, repeat, head_size)
        scores = block_scores(
            grouped, keys_all, visible(row_index, row_segment, index, segment), scale
        )
        peak = jnp.max(scores, axis=-1, keepdims=True)
        weights = jnp.exp(scores - peak)
        total = jnp.sum(weights, axis=-1, keepdims=True)
        probs = weights / total
        context_block = jnp.einsum(
            "krbt,tkd->bkrd",
            probs.astype(jnp.bfloat16),
            values_all,
            preferred_element_type=jnp.float32,
        )
        return (
            context_block.reshape(block, heads_local, head_size),
            (peak + jnp.log(total))[..., 0],
        )

    query_blocks = queries.reshape(blocks, block, heads_local, head_size)
    index_blocks = my_index.reshape(blocks, block)
    segment_blocks = my_segment.reshape(blocks, block)
    context, log_total = lax.map(attend, (query_blocks, index_blocks, segment_blocks))
    context = context.reshape(rows_narrow, heads_local, head_size)
    gate = jax.nn.sigmoid(gate_logit)
    gated = (context * gate[:, :, None]).astype(jnp.bfloat16).reshape(rows_narrow, query_cols)
    context_all, attention_term = contract(gated, output_weight, False)
    middle = inputs + attention_term
    inverse_two = lax.rsqrt(row_total(jnp.sum(middle * middle, axis=1)) / width_full + EPS)[:, None]
    hat_two = middle * inverse_two
    normed_two = (hat_two * gain_two).astype(jnp.bfloat16)
    gate_up_weight = jnp.concatenate([gate_weight, up_weight], axis=1)
    normed_two_all, gate_up = expand(normed_two, gate_up_weight, False)
    gate_pre = gate_up[:, :hidden_local]
    up_pre = gate_up[:, hidden_local:]
    hidden = (jax.nn.silu(gate_pre) * up_pre).astype(jnp.bfloat16)
    hidden_all, mlp_term = contract(hidden, down_weight, False)
    layer_output = (middle + mlp_term).astype(jnp.bfloat16)
    upstream_all, hidden_grad = expand(cotangent, down_weight, True)
    down_grad = dot_inner(hidden_all, upstream_all)
    gate_sigmoid = jax.nn.sigmoid(gate_pre)
    gate_grad = hidden_grad * up_pre * gate_sigmoid * (1.0 + gate_pre * (1.0 - gate_sigmoid))
    up_grad = hidden_grad * jax.nn.silu(gate_pre)
    gate_up_low = jnp.concatenate([gate_grad, up_grad], axis=1).astype(jnp.bfloat16)
    gate_up_all, normed_two_grad = contract(gate_up_low, gate_up_weight, True)
    gate_up_grad = dot_inner(normed_two_all, gate_up_all)
    gain_two_term = jnp.sum(normed_two_grad * hat_two, axis=0)
    scaled_two = normed_two_grad * gain_two
    inner_two = row_total(jnp.sum(scaled_two * hat_two, axis=1))[:, None] / width_full
    middle_grad = cotangent.astype(jnp.float32) + inverse_two * (scaled_two - hat_two * inner_two)
    middle_low = middle_grad.astype(jnp.bfloat16)
    middle_all, gated_grad = expand(middle_low, output_weight, True)
    output_grad = dot_inner(context_all, middle_all)
    gated_grad = gated_grad.reshape(rows_narrow, heads_local, head_size)
    context_grad = (gated_grad * gate[:, :, None]).astype(jnp.bfloat16)
    gate_logit_grad = jnp.sum(gated_grad * context, axis=2) * gate * (1.0 - gate)

    def attend_back(carry, block_inputs):
        key_sum, value_sum = carry
        query_block, grad_block, log_block, row_index, row_segment = block_inputs
        grouped = query_block.reshape(block, pair_heads, repeat, head_size)
        grad_grouped = grad_block.reshape(block, pair_heads, repeat, head_size)
        scores = block_scores(
            grouped, keys_all, visible(row_index, row_segment, index, segment), scale
        )
        probs = jnp.exp(scores - log_block[..., None])
        prob_grads = jnp.einsum(
            "bkrd,tkd->krbt", grad_grouped, values_all, preferred_element_type=jnp.float32
        )
        inner = jnp.sum(probs * prob_grads, axis=-1, keepdims=True)
        score_grads = (probs * (prob_grads - inner)).astype(jnp.bfloat16)
        query_part = (
            jnp.einsum("krbt,tkd->bkrd", score_grads, keys_all, preferred_element_type=jnp.float32)
            * scale
        )
        key_sum = (
            key_sum
            + jnp.einsum("krbt,bkrd->tkd", score_grads, grouped, preferred_element_type=jnp.float32)
            * scale
        )
        value_sum = value_sum + jnp.einsum(
            "krbt,bkrd->tkd",
            probs.astype(jnp.bfloat16),
            grad_grouped,
            preferred_element_type=jnp.float32,
        )
        return ((key_sum, value_sum), query_part.reshape(block, heads_local, head_size))

    empty = jnp.zeros((group_rows, pair_heads, head_size), jnp.float32)
    grad_blocks = context_grad.reshape(blocks, block, heads_local, head_size)
    (key_sum, value_sum), query_grads = lax.scan(
        attend_back,
        (empty, empty),
        (query_blocks, grad_blocks, log_total, index_blocks, segment_blocks),
    )
    query_grads = query_grads.reshape(rows_narrow, heads_local, head_size)
    key_mine, value_mine = (
        lax.psum_scatter(
            key_sum.astype(jnp.bfloat16), "narrow", scatter_dimension=0, tiled=True
        ).astype(jnp.float32),
        lax.psum_scatter(
            value_sum.astype(jnp.bfloat16), "narrow", scatter_dimension=0, tiled=True
        ).astype(jnp.float32),
    )
    query_raw_grad, query_gain_term = head_norm_back(
        rotate_back(query_grads, cosine, sine), query_hat, query_inverse, query_gain
    )
    key_raw_grad, key_gain_term = head_norm_back(
        rotate_back(key_mine, cosine, sine), key_hat, key_inverse, key_gain
    )
    joined_low = jnp.concatenate(
        [
            query_raw_grad.reshape(rows_narrow, query_cols),
            key_raw_grad.reshape(rows_narrow, key_cols),
            value_mine.reshape(rows_narrow, key_cols),
            gate_logit_grad,
        ],
        axis=1,
    ).astype(jnp.bfloat16)
    joined_all, normed_grad = contract(joined_low, joined_weight, True)
    joined_grad = dot_inner(normed_all, joined_all)
    gain_one_term = jnp.sum(normed_grad * hat_one, axis=0)
    scaled_one = normed_grad * gain_one
    inner_one = row_total(jnp.sum(scaled_one * hat_one, axis=1))[:, None] / width_full
    tokens_gradient = middle_grad + inverse_one * (scaled_one - hat_one * inner_one)
    joined_grad, output_grad, gate_up_grad, down_grad = (
        lax.psum(joined_grad.astype(jnp.bfloat16), "dp").astype(jnp.float32),
        lax.psum(output_grad.astype(jnp.bfloat16), "dp").astype(jnp.float32),
        lax.psum(gate_up_grad.astype(jnp.bfloat16), "dp").astype(jnp.float32),
        lax.psum(down_grad.astype(jnp.bfloat16), "dp").astype(jnp.float32),
    )
    gain_one_full = lax.dynamic_update_slice_in_dim(
        jnp.zeros_like(attention_gain), gain_one_term, narrow_index * width_local, 0
    )
    gain_two_full = lax.dynamic_update_slice_in_dim(
        jnp.zeros_like(feedforward_gain), gain_two_term, narrow_index * width_local, 0
    )
    gain_one_full, gain_two_full, query_gain_term, key_gain_term = lax.psum(
        (gain_one_full, gain_two_full, query_gain_term, key_gain_term), ("dp", "wide", "narrow")
    )
    query_gradient = joined_grad[:, :query_cols]
    key_gradient = joined_grad[:, query_cols : query_cols + key_cols]
    value_gradient = joined_grad[:, query_cols + key_cols : query_cols + 2 * key_cols]
    head_gate_gradient = joined_grad[:, query_cols + 2 * key_cols :]
    gate_gradient = gate_up_grad[:, :hidden_local]
    up_gradient = gate_up_grad[:, hidden_local:]
    return (
        layer_output,
        tokens_gradient,
        gain_one_full,
        query_gradient,
        key_gradient,
        value_gradient,
        head_gate_gradient,
        query_gain_term,
        key_gain_term,
        output_grad,
        gain_two_full,
        gate_gradient,
        up_gradient,
        down_grad,
    )


def solution(mesh):
    return jax.shard_map(
        on_device,
        mesh=mesh,
        in_specs=(
            P(("dp", "wide"), "narrow"),
            P("dp", None),
            P(),
            P("narrow", "wide"),
            P("narrow", "wide"),
            P("narrow", "wide"),
            P("narrow", "wide"),
            P(),
            P(),
            P("wide", "narrow"),
            P(),
            P("narrow", "wide"),
            P("narrow", "wide"),
            P("wide", "narrow"),
            P(("dp", "wide"), "narrow"),
        ),
        out_specs=(
            P(("dp", "wide"), "narrow"),
            P(("dp", "wide"), "narrow"),
            P(),
            P("narrow", "wide"),
            P("narrow", "wide"),
            P("narrow", "wide"),
            P("narrow", "wide"),
            P(),
            P(),
            P("wide", "narrow"),
            P(),
            P("narrow", "wide"),
            P("narrow", "wide"),
            P("wide", "narrow"),
        ),
        check_vma=False,
    )
```

profile of v0, /device:TPU:0, one launch (start us, length us, event | category | flops | bytes accessed | tf_op | source)
XLA Modules:
  0.0 2702.8 jit_solution(11104213106023687378)
XLA Ops:
  21.5 80.9 %all-gather.11.cloned.1.call-done = bf16[4096,512]{1,0:T(8,128)(2,1)} async-done(((bf16[1024,512]{1,0:T(8,128)(2,1)}), bf16[4096,512]{1,0:T(8,128)(2,1)}) %all-gather.11.cloned.1.call-update) | async-done | bytes 4194320 | tf_op jit(solution)/shard_map/all_gather | solution.py:28
  117.1 122.4 %reduce-scatter.11.cloned.1.call-done = f32[1024,1028]{0,1:T(8,128)} async-done(((f32[4096,1028]{0,1:T(8,128)}), f32[1024,1028]{0,1:T(8,128)}) %reduce-scatter.11.cloned.1.call-update) | async-done | bytes 4210704 | tf_op jit(solution)/shard_map/reduce_scatter | solution.py:37
  272.0 18.6 all-gather.15.cloned.1.call-done
  290.6 100.4 %while.28 = (s32[]{:T(128)}, f32[2,512,4,128]{3,1,2,0:T(8,128)}, f32[2,2,2,512]{3,2,1,0:T(2,128)S(1)}, s32[2,512]{1,0:T(2,128)S(1)}, s32[4096]{0:T(1024)S(1)}, /...) while((s32[]{:T(128)}, f32[2,512,4,128]{3,1,2,0:T(8,128)}, ...), condition=%wide.region_11.12_spmd.clone, body=%wide.region_8.11_spmd.clone.sunk | while | flops 4404021248 | bytes 134860992 | solution.py:209
  323.9 15.7 fusion.136
  397.0 34.2 %all-gather.17.cloned.1.call-done = bf16[4096,512]{1,0:T(8,128)(2,1)} async-done(((bf16[1024,512]{1,0:T(8,128)(2,1)}), bf16[4096,512]{1,0:T(8,128)(2,1)}) %all-gather.17.cloned.1.call-update) | async-done | bytes 4194320 | tf_op jit(solution)/shard_map/all_gather | solution.py:42
  440.6 143.2 %reduce-scatter.13.cloned.1.call-done = f32[1024,512]{1,0:T(8,128)} async-done(((f32[4096,512]{1,0:T(8,128)}), f32[1024,512]{1,0:T(8,128)}) %reduce-scatter.13.cloned.1.call-update) | async-done | bytes 2097168 | tf_op jit(solution)/shard_map/reduce_scatter | solution.py:51
  596.3 70.5 %all-gather.23.cloned.1.call-done = bf16[4096,512]{1,0:T(8,128)(2,1)} async-done(((bf16[1024,512]{1,0:T(8,128)(2,1)}), bf16[4096,512]{1,0:T(8,128)(2,1)}) %all-gather.23.cloned.1.call-update) | async-done | bytes 4194320 | tf_op jit(solution)/shard_map/all_gather | solution.py:28
  685.5 62.6 %all-gather.19.cloned.1.call-done = bf16[4096,512]{1,0:T(8,128)(2,1)} async-done(((bf16[1024,512]{1,0:T(8,128)(2,1)}), bf16[4096,512]{1,0:T(8,128)(2,1)}) %all-gather.19.cloned.1.call-update) | async-done | bytes 4194320 | tf_op jit(solution)/shard_map/all_gather | solution.py:28
  748.1 36.5 %fusion.76 = f32[4096,3072]{1,0:T(8,128)} fusion(bf16[4096,512]{1,0:T(8,128)(2,1)} %all-gather.19.cloned.1.call-done, bf16[512,3072]{1,0:T(8,128)(2,1)} %constant_dynamic-update-slice_fusion.2), kind=kOutput, calls=%fused_computation.169 | convolution fusion | flops 12884901888 | bytes 57671680 | tf_op jit(solution)/shard_map/dot_general | solution.py:12
  784.9 146.3 %reduce-scatter.19.cloned.1.call-done = f32[1024,1536]{1,0:T(8,128)} async-done(((f32[4096,1536]{1,0:T(8,128)}), f32[1024,1536]{1,0:T(8,128)}) %reduce-scatter.19.cloned.1.call-update) | async-done | bytes 6291472 | tf_op jit(solution)/shard_map/reduce_scatter | solution.py:37
  931.2 349.0 %reduce-scatter.15.cloned.1.call-done = f32[1024,3072]{1,0:T(8,128)} async-done(((f32[4096,3072]{1,0:T(8,128)}), f32[1024,3072]{1,0:T(8,128)}) %reduce-scatter.15.cloned.1.call-update) | async-done | bytes 12582928 | tf_op jit(solution)/shard_map/reduce_scatter | solution.py:37
  1293.5 154.9 %all-gather.25.cloned.1.call-done = bf16[4096,3072]{1,0:T(8,128)(2,1)} async-done(((bf16[1024,3072]{1,0:T(8,128)(2,1)}), bf16[4096,3072]{1,0:T(8,128)(2,1)}) %all-gather.25.cloned.1.call-update) | async-done | bytes 25165840 | tf_op jit(solution)/shard_map/all_gather | solution.py:42
  1448.4 21.0 fusion.79
  1469.4 144.7 %reduce-scatter.21.cloned.1.call-done = f32[1024,512]{1,0:T(8,128)} async-done(((f32[4096,512]{1,0:T(8,128)}), f32[1024,512]{1,0:T(8,128)}) %reduce-scatter.21.cloned.1.call-update) | async-done | bytes 2097168 | tf_op jit(solution)/shard_map/reduce_scatter | solution.py:51
  1628.2 81.2 %all-gather.27.cloned.1.call-done = bf16[4096,512]{1,0:T(8,128)(2,1)} async-done(((bf16[1024,512]{1,0:T(8,128)(2,1)}), bf16[4096,512]{1,0:T(8,128)(2,1)}) %all-gather.27.cloned.1.call-update) | async-done | bytes 4194320 | tf_op jit(solution)/shard_map/all_gather | solution.py:28
  1717.3 70.0 %reduce-scatter.23.cloned.1.call-done = f32[1024,512]{1,0:T(8,128)} async-done(((f32[4096,512]{1,0:T(8,128)}), f32[1024,512]{1,0:T(8,128)}) %reduce-scatter.23.cloned.1.call-update) | async-done | bytes 2097168 | tf_op jit(solution)/shard_map/reduce_scatter | solution.py:37
  1793.1 223.9 %while.29 = (s32[]{:T(128)}, f32[4096,2,128]{0,2,1:T(8,128)}, f32[4096,2,128]{0,2,1:T(8,128)}, f32[2,512,4,128]{3,1,0,2:T(8,128)}, bf16[2,512,4,128]{3,1,2,0:T(8...) while((s32[]{:T(128)}, f32[4096,2,128]{0,2,1:T(8,128)}, ...), condition=%wide.region_24.25_spmd.clone, body=%wide.region_22.24_spmd.clone.sunk | while | flops 10877143040 | bytes 349286720 | solution.py:277
  1811.8 17.4 fusion.151
  1829.2 25.2 fusion.148
  1854.3 28.4 %fusion.149 = bf16[2,2,512,4096]{3,2,1,0:T(8,128)(2,1)} fusion(f32[2,512,2,4096]{3,1,2,0:T(8,128)} %get-tuple-element.583, f32[2,512,2,4096]{3,1,2,0:T(8,128)} %fusion.146, f32[2,2,512]{2,1,0:T(2,128)S(1)} %get-tuple-element.584, f32[2,2,512]{2,1,0:T(2,128)S(1)} %dynamic-slice_bitcast_fusion.2, pred[512,4096]{1,0:T(8,128)(4,1)} %fusion.147), kind=kLoop, calls=%fused_computation.26.clone.1 | loop fusion | flops 50331648 | bytes 85999616 | tf_op jit(solution)/shard_map/while/body/eval_jaxpr/convert_element_type | solution.py:257
  1922.9 18.5 fusion.151
  1941.4 25.2 fusion.148
  1966.6 28.4 %fusion.149 = bf16[2,2,512,4096]{3,2,1,0:T(8,128)(2,1)} fusion(f32[2,512,2,4096]{3,1,2,0:T(8,128)} %get-tuple-element.583, f32[2,512,2,4096]{3,1,2,0:T(8,128)} %fusion.146, f32[2,2,512]{2,1,0:T(2,128)S(1)} %get-tuple-element.584, f32[2,2,512]{2,1,0:T(2,128)S(1)} %dynamic-slice_bitcast_fusion.2, pred[512,4096]{1,0:T(8,128)(4,1)} %fusion.147), kind=kLoop, calls=%fused_computation.26.clone.1 | loop fusion | flops 50331648 | bytes 85999616 | tf_op jit(solution)/shard_map/while/body/eval_jaxpr/convert_element_type | solution.py:257
  2056.6 29.1 %reduce-scatter.27.cloned.1.call-done = bf16[1024,2,128]{0,2,1:T(8,128)(2,1)} async-done(((bf16[4096,2,128]{0,2,1:T(8,128)(2,1)}), bf16[1024,2,128]{0,2,1:T(8,128)(2,1)}) %reduce-scatter.27.cloned.1.call-update) | async-done | bytes 524304 | tf_op jit(solution)/shard_map/reduce_scatter | solution.py:287
  2088.3 81.5 %all-gather.21.cloned.1.call-done = bf16[4096,1536]{1,0:T(8,128)(2,1)} async-done(((bf16[1024,1536]{1,0:T(8,128)(2,1)}), bf16[4096,1536]{1,0:T(8,128)(2,1)}) %all-gather.21.cloned.1.call-update) | async-done | bytes 12582928 | tf_op jit(solution)/shard_map/all_gather | solution.py:42
  2181.7 20.8 convolution_convert_fusion
  2205.7 24.7 all-gather.29.cloned.1.call-done
  2266.7 127.6 %all-reduce.4.cloned.1.call-done = (bf16[512,1028]{0,1:T(8,128)(2,1)}, bf16[512,3072]{1,0:T(8,128)(2,1)}, bf16[512,512]{1,0:T(8,128)(2,1)}, bf16[1536,512]{1,0:T(8,128)(2,1)}) async-done(((bf16[512,1028]{0,1:T(8,128)(2,1)}, bf16[512,3072]{1,0:T(8,128)(2,1)}, bf16[512,512]{1,0:T(8,128)(2,1)}, bf16[1536,512]{1,0:T(8,128)(2,1)}), (bf16[512,1028]{0,1:T(8,128)(2,1)}, bf16[512,3072]{1,0:T(8,128)(2,1)}, ...) | async-done | bytes 6295568 | tf_op jit(solution)/shard_map/psum | solution.py:313
  2410.7 131.0 %reduce-scatter.29.cloned.1.call-done = f32[1024,512]{1,0:T(8,128)} async-done(((f32[4096,512]{1,0:T(8,128)}), f32[1024,512]{1,0:T(8,128)}) %reduce-scatter.29.cloned.1.call-update) | async-done | bytes 2097168 | tf_op jit(solution)/shard_map/reduce_scatter | solution.py:51
  2544.3 46.1 %all-reduce = (f32[2048]{0:T(1024)}, f32[128]{0:T(128)}, f32[128]{0:T(128)}, f32[2048]{0:T(1024)}) all-reduce(f32[2048]{0:T(1024)S(1)} %dynamic_update_slice.17, f32[128]{0:T(128)S(1)} %bitcast_reduce_fusion.1, f32[128]{0:T(128)S(1)} %bitcast_reduce_fusion.2, ...), channel_id=1, replica_groups=mesh['dp'=2,'wide'=4,'narrow'=4] {'dp','wide','narrow'}, use_global_device_ids=true, to_apply=%region_34.35 | all-reduce | flops 4352 | bytes 34816 | tf_op jit(solution)/shard_map/psum | solution.py:324
  2596.6 93.6 %reduce-scatter.17.cloned.1.call-done = f32[1024,512]{1,0:T(8,128)} async-done(((f32[4096,512]{1,0:T(8,128)}), f32[1024,512]{1,0:T(8,128)}) %reduce-scatter.17.cloned.1.call-update) | async-done | bytes 2097168 | tf_op jit(solution)/shard_map/reduce_scatter | solution.py:51
  (330 shorter events, 437.6 us)
Async XLA Ops:
  7.2 659.6 %copy-start = (bf16[1536,512]{1,0:T(8,128)(2,1)S(1)}, bf16[1536,512]{1,0:T(8,128)(2,1)}, u32[]{:S(2)}) copy-start(bf16[1536,512]{1,0:T(8,128)(2,1)} %param.32) | copy-start | bytes 4718596
  7.2 95.2 %all-gather.11.cloned.1.call-start = ((), (), s32[]{:S(2)}) async-start(), calls=%async_computation.10 | async-start | bytes 5242880 | tf_op jit(solution)/shard_map/all_gather | solution.py:28
  21.2 218.3 %reduce-scatter.11.cloned.1.call-start = ((), (), s32[]{:S(2)}) async-start(), calls=%async_computation.11 | async-start | bytes 21135360 | tf_op jit(solution)/shard_map/reduce_scatter | solution.py:37
  115.0 152.9 %all-gather.13.cloned.1.call-start = ((), (), s32[]{:S(2)}) async-start(), calls=%async_computation.12 | async-start | bytes 2621440 | tf_op jit(solution)/shard_map/all_gather | solution.py:181
  243.3 47.3 %all-gather.15.cloned.1.call-start = ((), (), s32[]{:S(2)}) async-start(), calls=%async_computation.13 | async-start | bytes 2621440 | tf_op jit(solution)/shard_map/all_gather | solution.py:182
  245.7 185.5 %all-gather.17.cloned.1.call-start = ((), (), s32[]{:S(2)}) async-start(), calls=%async_computation.14 | async-start | bytes 5242880 | tf_op jit(solution)/shard_map/all_gather | solution.py:42
  396.6 187.2 %reduce-scatter.13.cloned.1.call-start = ((), (), s32[]{:S(2)}) async-start(), calls=%async_computation.15 | async-start | bytes 10485760 | tf_op jit(solution)/shard_map/reduce_scatter | solution.py:51
  439.0 144.8 %copy-start.6 = (bf16[1024,512]{1,0:T(8,128)(2,1)S(1)}, bf16[1024,512]{1,0:T(8,128)(2,1)}, u32[]{:S(2)}) copy-start(bf16[1024,512]{1,0:T(8,128)(2,1)} %param.19) | copy-start | bytes 3145732
  439.0 227.7 %all-gather.23.cloned.1.call-start = ((), (), s32[]{:S(2)}) async-start(), calls=%async_computation.20 | async-start | bytes 5242880 | tf_op jit(solution)/shard_map/all_gather | solution.py:28
  439.8 308.4 %all-gather.19.cloned.1.call-start = ((), (), s32[]{:S(2)}) async-start(), calls=%async_computation.16 | async-start | bytes 5242880 | tf_op jit(solution)/shard_map/all_gather | solution.py:28
  440.6 1183.1 %copy-start.44 = (f32[512]{0:T(512)}, f32[512]{0:T(512)S(1)}, u32[]{:S(2)}) copy-start(f32[512]{0:T(512)S(1)} %dynamic_slice.46) | copy-start | bytes 6148
  593.1 1030.6 %copy-start.40 = (f32[1024]{0:T(1024)}, f32[1024]{0:T(1024)S(1)}, u32[]{:S(2)}) copy-start(f32[1024]{0:T(1024)S(1)} %add_rsqrt_fusion.2) | copy-start | bytes 12292
  596.2 335.0 %reduce-scatter.19.cloned.1.call-start = ((), (), s32[]{:S(2)}) async-start(), calls=%async_computation.21 | async-start | bytes 31457280 | tf_op jit(solution)/shard_map/reduce_scatter | solution.py:37
  681.4 598.7 %reduce-scatter.15.cloned.1.call-start = ((), (), s32[]{:S(2)}) async-start(), calls=%async_computation.17 | async-start | bytes 62914560 | tf_op jit(solution)/shard_map/reduce_scatter | solution.py:37
  784.7 663.7 %all-gather.25.cloned.1.call-start = ((), (), s32[]{:S(2)}) async-start(), calls=%async_computation.22 | async-start | bytes 31457280 | tf_op jit(solution)/shard_map/all_gather | solution.py:42
  1293.4 320.7 %reduce-scatter.21.cloned.1.call-start = ((), (), s32[]{:S(2)}) async-start(), calls=%async_computation.23 | async-start | bytes 10485760 | tf_op jit(solution)/shard_map/reduce_scatter | solution.py:51
  1469.4 155.0 %copy-start.11 = (bf16[1024,512]{1,0:T(8,128)(2,1)S(1)}, bf16[1024,512]{1,0:T(8,128)(2,1)}, u32[]{:S(2)}) copy-start(bf16[1024,512]{1,0:T(8,128)(2,1)} %param.33) | copy-start | bytes 3145732
  1469.4 240.0 %all-gather.27.cloned.1.call-start = ((), (), s32[]{:S(2)}) async-start(), calls=%async_computation.24 | async-start | bytes 5242880 | tf_op jit(solution)/shard_map/all_gather | solution.py:28
  1628.1 159.2 %reduce-scatter.23.cloned.1.call-start = ((), (), s32[]{:S(2)}) async-start(), calls=%async_computation.25 | async-start | bytes 10485760 | tf_op jit(solution)/shard_map/reduce_scatter | solution.py:37
  1717.2 334.9 %reduce-scatter.25.cloned.1.call-start = ((), (), s32[]{:S(2)}) async-start(), calls=%async_computation.26 | async-start | bytes 2621440 | tf_op jit(solution)/shard_map/reduce_scatter | solution.py:284
  2020.8 64.9 %reduce-scatter.27.cloned.1.call-start = ((), (), s32[]{:S(2)}) async-start(), calls=%async_computation.27 | async-start | bytes 2621440 | tf_op jit(solution)/shard_map/reduce_scatter | solution.py:287
  2024.7 145.1 %all-gather.21.cloned.1.call-start = ((), (), s32[]{:S(2)}) async-start(), calls=%async_computation.18 | async-start | bytes 15728640 | tf_op jit(solution)/shard_map/all_gather | solution.py:42
  2025.3 205.2 %all-gather.29.cloned.1.call-start = ((), (), s32[]{:S(2)}) async-start(), calls=%async_computation.28 | async-start | bytes 10567680 | tf_op jit(solution)/shard_map/all_gather | solution.py:42
  2088.3 306.0 %all-reduce.4.cloned.1.call-start = ((), (), s32[]{:S(2)}) async-start(), calls=%async_computation.30 | async-start | bytes 12599296 | tf_op jit(solution)/shard_map/psum | solution.py:313
  2240.7 301.0 %reduce-scatter.29.cloned.1.call-start = ((), (), s32[]{:S(2)}) async-start(), calls=%async_computation.29 | async-start | bytes 10485760 | tf_op jit(solution)/shard_map/reduce_scatter | solution.py:51
  2254.1 436.1 %reduce-scatter.17.cloned.1.call-start = ((), (), s32[]{:S(2)}) async-start(), calls=%async_computation.19 | async-start | bytes 10485760 | tf_op jit(solution)/shard_map/reduce_scatter | solution.py:51
  2407.1 134.6 %copy-start.7 = (bf16[1024,512]{1,0:T(8,128)(2,1)S(1)}, bf16[1024,512]{1,0:T(8,128)(2,1)}, u32[]{:S(2)}) copy-start(bf16[1024,512]{1,0:T(8,128)(2,1)} %param.19) | copy-start | bytes 3145732
  2407.1 134.6 %copy-start.43 = (f32[1024]{0:T(1024)S(1)}, f32[1024]{0:T(1024)}, u32[]{:S(2)}) copy-start(f32[1024]{0:T(1024)} %copy-done.42) | copy-start | bytes 12292
  2407.1 134.6 %copy-start.49 = (f32[512]{0:T(512)S(1)}, f32[512]{0:T(512)}, u32[]{:S(2)}) copy-start(f32[512]{0:T(512)} %copy-done.48) | copy-start | bytes 6148
  2410.7 279.6 %copy-start.41 = (f32[1024]{0:T(1024)S(1)}, f32[1024]{0:T(1024)}, u32[]{:S(2)}) copy-start(f32[1024]{0:T(1024)} %copy-done.40) | copy-start | bytes 12292
  2410.7 279.6 %copy-start.45 = (f32[512]{0:T(512)S(1)}, f32[512]{0:T(512)}, u32[]{:S(2)}) copy-start(f32[512]{0:T(512)} %copy-done.44) | copy-start | bytes 6148
  2410.7 279.6 %copy-start.47 = (f32[1024]{0:T(1024)S(1)}, f32[1024]{0:T(1024)}, u32[]{:S(2)}) copy-start(f32[1024]{0:T(1024)} %copy-done.46) | copy-start | bytes 12292
  (60 other events, 1155.9 us)
Sparse Core Ops, SparseCore 0:
  21.4 81.0 all-gather.10
  115.2 124.2 reduce-scatter.10
  243.4 22.5 all-gather.12
  268.0 22.5 all-gather.14
  396.7 34.4 all-gather.16
  439.1 144.6 reduce-scatter.12
  585.4 81.3 all-gather.22
  668.9 79.2 all-gather.18
  750.7 180.4 reduce-scatter.18
  933.6 346.4 reduce-scatter.14
  1293.5 154.7 all-gather.24
  1469.5 144.6 reduce-scatter.20
  1628.2 81.0 all-gather.26
  1717.3 69.9 reduce-scatter.22
  2020.9 31.1 reduce-scatter.24
  2054.5 31.1 reduce-scatter.26
  2087.7 82.0 all-gather.20
  2171.8 58.6 all-gather.28
  2240.8 153.4 all-reduce.3
  2396.5 145.1 reduce-scatter.28
  2544.1 146.1 reduce-scatter.16
where the time goes:
time: 2710 us; the launch traced here: 2700 us
  waiting for transfers between devices  1980 us (73%)
  matrix products  380 us (14%)
  other arithmetic  184 us (7%)
  blocking collectives  73.1 us (3%)
  local copies, waits for them, and re-layouts  70.3 us (3%)
    reduce_scatter x4, waiting for transfers between devices, expand(): lax.psum_scatter(expand_partial_term(), 'narrow', scatter_dimension=0, ti...  688 us
    reduce_scatter x4, waiting for transfers between devices, contract(): lax.psum_scatter(contract_partial_term(), 'wide', scatter_dimension=0, ti...  513 us
    all_gather x4, waiting for transfers between devices, contract(): gathered = lax.all_gather(local_rows, 'narrow', axis=0, tiled=True)  295 us
    all_gather x4, waiting for transfers between devices, expand(): gathered = lax.all_gather(local_rows, 'wide', axis=0, tiled=True)  295 us
    psum x1, waiting for transfers between devices, on_device(): lax.psum(joined_grad.astype(jnp.bfloat16), 'dp').astype(jnp.float32)  128 us
    dot_general x4, matrix products, dot_rows(): return jnp.dot(left, right, preferred_element_type=jnp.float32)  68.6 us
    convert_element_type x2, other arithmetic, attend_back(): score_grads = (probs * (prob_grads - inner)).astype(jnp.bfloat16)  56.9 us
    dot_general x4, matrix products, dot_trans(): lax.dot_general(left, right, (((1,), (1,)), ((), ())), preferred_element_...  55.7 us
  transfers between devices with their start and end apart: 21, of which 20 were waited for; matrix products, arithmetic and copies ran while one was open for 7% of the time, Pallas kernels for 0%

commit v1 on v0

--- a/solution.py
+++ b/solution.py
@@ -25,7 +25,9 @@
 
 
 def expand(local_rows, weight, transpose):
-    gathered = lax.all_gather(local_rows, "wide", axis=0, tiled=True)
+    gathered = jnp.concatenate(
+        lax.all_to_all(jnp.stack([local_rows] * lax.axis_size("wide")), "wide", 0, 0), axis=0
+    )
 
     def expand_partial_term():
         if transpose:

time: 2710 us -> 2670 us (0.985)
  waiting for transfers between devices: 1980 us -> 1620 us
  blocking collectives: 73.1 us -> 377 us
    all_to_all x0 -> x2, blocking collectives: none -> 305 us  [expand(): lax.all_to_all(jnp.stack([local_rows] * lax.axis_size('wide')), 'wide', 0...]
    all_gather x4 -> x0, waiting for transfers between devices: 295 us -> none  [expand(): gathered = lax.all_gather(local_rows, 'wide', axis=0, tiled=True)]
    all_to_all x0 -> x2, waiting for transfers between devices: none -> 180 us  [expand(): lax.all_to_all(jnp.stack([local_rows] * lax.axis_size('wide')), 'wide', 0...]
    reduce_scatter x4, waiting for transfers between devices: 513 us -> 373 us  [contract(): lax.psum_scatter(contract_partial_term(), 'wide', scatter_dimension=0, ti...]
    reduce_scatter x4, waiting for transfers between devices: 688 us -> 588 us  [expand(): lax.psum_scatter(expand_partial_term(), 'narrow', scatter_dimension=0, ti...]
  transfers between devices with their start and end apart: 21 -> 19, of which waited for: 20 -> 18; matrix products, arithmetic and copies ran while one was open for 7% -> 7% of each run, Pallas kernels for 0% -> 0%
where the time goes in v1:
time: 2670 us; the launch traced here: 2660 us
  waiting for transfers between devices  1620 us (61%)
  blocking collectives  377 us (14%)
  matrix products  365 us (14%)
  other arithmetic  181 us (7%)
  local copies, waits for them, and re-layouts  81.7 us (3%)
    reduce_scatter x4, waiting for transfers between devices, expand(): lax.psum_scatter(expand_partial_term(), 'narrow', scatter_dimension=0, ti...  588 us
    reduce_scatter x4, waiting for transfers between devices, contract(): lax.psum_scatter(contract_partial_term(), 'wide', scatter_dimension=0, ti...  373 us
    all_to_all x2, blocking collectives, expand(): lax.all_to_all(jnp.stack([local_rows] * lax.axis_size('wide')), 'wide', 0...  305 us
    all_gather x4, waiting for transfers between devices, contract(): gathered = lax.all_gather(local_rows, 'narrow', axis=0, tiled=True)  294 us
    all_to_all x2, waiting for transfers between devices, expand(): lax.all_to_all(jnp.stack([local_rows] * lax.axis_size('wide')), 'wide', 0...  180 us
    psum x1, waiting for transfers between devices, on_device(): lax.psum(joined_grad.astype(jnp.bfloat16), 'dp').astype(jnp.float32)  128 us
    dot_general x4, matrix products, dot_rows(): return jnp.dot(left, right, preferred_element_type=jnp.float32)  58.1 us
    convert_element_type x2, other arithmetic, attend_back(): score_grads = (probs * (prob_grads - inner)).astype(jnp.bfloat16)  56.8 us
  transfers between devices with their start and end apart: 19, of which 18 were waited for; matrix products, arithmetic and copies ran while one was open for 7% of the time, Pallas kernels for 0%

profile of v1, /device:TPU:0, one launch (start us, length us, event | category | flops | bytes accessed | tf_op | source)
XLA Modules:
  0.0 2661.1 jit_solution(10547921357251735126)
XLA Ops:
  27.7 91.9 %all-to-all-done = bf16[4,1024,512]{2,1,0:T(8,128)(2,1)} async-done(((bf16[4,1024,512]{2,1,0:T(8,128)(2,1)}), bf16[4,1024,512]{2,1,0:T(8,128)(2,1)}, u32[]{:S(2)}, u32[]{:S(2)}) %all-to-all-start) | async-done | bytes 4194336 | tf_op jit(solution)/shard_map/all_to_all | solution.py:29
  134.2 123.2 %reduce-scatter.11.cloned.1.call-done = f32[1024,1028]{0,1:T(8,128)} async-done(((f32[4096,1028]{0,1:T(8,128)}), f32[1024,1028]{0,1:T(8,128)}) %reduce-scatter.11.cloned.1.call-update) | async-done | bytes 4210704 | tf_op jit(solution)/shard_map/reduce_scatter | solution.py:39
  290.2 18.4 all-gather.9.cloned.1.call-done
  308.6 100.4 %while.28 = (s32[]{:T(128)}, f32[2,512,4,128]{3,1,2,0:T(8,128)}, f32[2,2,2,512]{3,2,1,0:T(2,128)S(1)}, s32[2,512]{1,0:T(2,128)S(1)}, s32[4096]{0:T(1024)S(1)}, /...) while((s32[]{:T(128)}, f32[2,512,4,128]{3,1,2,0:T(8,128)}, ...), condition=%wide.region_11.12_spmd.clone, body=%wide.region_8.11_spmd.clone.sunk | while | flops 4404021248 | bytes 134860992 | solution.py:211
  342.0 15.8 fusion.136
  392.2 15.8 fusion.136
  414.8 34.4 %all-gather.11.cloned.1.call-done = bf16[4096,512]{1,0:T(8,128)(2,1)} async-done(((bf16[1024,512]{1,0:T(8,128)(2,1)}), bf16[4096,512]{1,0:T(8,128)(2,1)}) %all-gather.11.cloned.1.call-update) | async-done | bytes 4194320 | tf_op jit(solution)/shard_map/all_gather | solution.py:44
  458.6 207.7 %all_to_all.20 = bf16[4,1024,512]{2,1,0:T(8,128)(2,1)S(1)} all-to-all(bf16[4,1024,512]{2,1,0:T(8,128)(2,1)S(1)} %stack.10), channel_id=1, replica_groups=mesh['dp'=2,'wide'=4,'narrow'=4] {'wide'}, dimensions={0} | all-to-all | bytes 8388608 | tf_op jit(solution)/shard_map/all_to_all | solution.py:29
  714.2 88.3 %all-to-all-done.1 = bf16[4,1024,512]{2,1,0:T(8,128)(2,1)} async-done(((bf16[4,1024,512]{2,1,0:T(8,128)(2,1)}), bf16[4,1024,512]{2,1,0:T(8,128)(2,1)}, u32[]{:S(2)}, u32[]{:S(2)}) %all-to-all-start.1) | async-done | bytes 4194336 | tf_op jit(solution)/shard_map/all_to_all | solution.py:29
  802.5 26.1 fusion.76
  828.7 45.8 %reduce-scatter.19.cloned.1.call-done = f32[1024,1536]{1,0:T(8,128)} async-done(((f32[4096,1536]{1,0:T(8,128)}), f32[1024,1536]{1,0:T(8,128)}) %reduce-scatter.19.cloned.1.call-update) | async-done | bytes 6291472 | tf_op jit(solution)/shard_map/reduce_scatter | solution.py:39
  874.4 349.1 %reduce-scatter.15.cloned.1.call-done = f32[1024,3072]{1,0:T(8,128)} async-done(((f32[4096,3072]{1,0:T(8,128)}), f32[1024,3072]{1,0:T(8,128)}) %reduce-scatter.15.cloned.1.call-update) | async-done | bytes 12582928 | tf_op jit(solution)/shard_map/reduce_scatter | solution.py:39
  1237.3 154.4 %all-gather.15.cloned.1.call-done = bf16[4096,3072]{1,0:T(8,128)(2,1)} async-done(((bf16[1024,3072]{1,0:T(8,128)(2,1)}), bf16[4096,3072]{1,0:T(8,128)(2,1)}) %all-gather.15.cloned.1.call-update) | async-done | bytes 25165840 | tf_op jit(solution)/shard_map/all_gather | solution.py:44
  1391.7 21.0 fusion.79
  1412.8 144.7 %reduce-scatter.21.cloned.1.call-done = f32[1024,512]{1,0:T(8,128)} async-done(((f32[4096,512]{1,0:T(8,128)}), f32[1024,512]{1,0:T(8,128)}) %reduce-scatter.21.cloned.1.call-update) | async-done | bytes 2097168 | tf_op jit(solution)/shard_map/reduce_scatter | solution.py:53
  1570.8 96.8 %all_to_all.21 = bf16[4,1024,512]{2,1,0:T(8,128)(2,1)S(1)} all-to-all(bf16[4,1024,512]{2,1,0:T(8,128)(2,1)S(1)} %stack.11), channel_id=1, replica_groups=mesh['dp'=2,'wide'=4,'narrow'=4] {'wide'}, dimensions={0} | all-to-all | bytes 8388608 | tf_op jit(solution)/shard_map/all_to_all | solution.py:29
  1675.5 70.5 %reduce-scatter.23.cloned.1.call-done = f32[1024,512]{1,0:T(8,128)} async-done(((f32[4096,512]{1,0:T(8,128)}), f32[1024,512]{1,0:T(8,128)}) %reduce-scatter.23.cloned.1.call-update) | async-done | bytes 2097168 | tf_op jit(solution)/shard_map/reduce_scatter | solution.py:39
  1751.8 223.9 %while.29 = (s32[]{:T(128)}, f32[4096,2,128]{0,2,1:T(8,128)}, f32[4096,2,128]{0,2,1:T(8,128)}, f32[2,512,4,128]{3,1,0,2:T(8,128)}, bf16[2,512,4,128]{3,1,2,0:T(8...) while((s32[]{:T(128)}, f32[4096,2,128]{0,2,1:T(8,128)}, ...), condition=%wide.region_24.25_spmd.clone, body=%wide.region_22.24_spmd.clone.sunk | while | flops 10877143040 | bytes 349286720 | solution.py:279
  1770.2 17.4 fusion.151
  1787.7 25.2 fusion.148
  1812.8 28.4 %fusion.149 = bf16[2,2,512,4096]{3,2,1,0:T(8,128)(2,1)} fusion(f32[2,512,2,4096]{3,1,2,0:T(8,128)} %get-tuple-element.583, f32[2,512,2,4096]{3,1,2,0:T(8,128)} %fusion.146, f32[2,2,512]{2,1,0:T(2,128)S(1)} %get-tuple-element.584, f32[2,2,512]{2,1,0:T(2,128)S(1)} %dynamic-slice_bitcast_fusion.2, pred[512,4096]{1,0:T(8,128)(4,1)} %fusion.147), kind=kLoop, calls=%fused_computation.26.clone.1 | loop fusion | flops 50331648 | bytes 85999616 | tf_op jit(solution)/shard_map/while/body/eval_jaxpr/convert_element_type | solution.py:259
  1881.4 18.5 fusion.151
  1899.9 25.2 fusion.148
  1925.1 28.4 %fusion.149 = bf16[2,2,512,4096]{3,2,1,0:T(8,128)(2,1)} fusion(f32[2,512,2,4096]{3,1,2,0:T(8,128)} %get-tuple-element.583, f32[2,512,2,4096]{3,1,2,0:T(8,128)} %fusion.146, f32[2,2,512]{2,1,0:T(2,128)S(1)} %get-tuple-element.584, f32[2,2,512]{2,1,0:T(2,128)S(1)} %dynamic-slice_bitcast_fusion.2, pred[512,4096]{1,0:T(8,128)(4,1)} %fusion.147), kind=kLoop, calls=%fused_computation.26.clone.1 | loop fusion | flops 50331648 | bytes 85999616 | tf_op jit(solution)/shard_map/while/body/eval_jaxpr/convert_element_type | solution.py:259
  2015.3 29.1 %reduce-scatter.27.cloned.1.call-done = bf16[1024,2,128]{0,2,1:T(8,128)(2,1)} async-done(((bf16[4096,2,128]{0,2,1:T(8,128)(2,1)}), bf16[1024,2,128]{0,2,1:T(8,128)(2,1)}) %reduce-scatter.27.cloned.1.call-update) | async-done | bytes 524304 | tf_op jit(solution)/shard_map/reduce_scatter | solution.py:289
  2047.0 81.6 %all-gather.13.cloned.1.call-done = bf16[4096,1536]{1,0:T(8,128)(2,1)} async-done(((bf16[1024,1536]{1,0:T(8,128)(2,1)}), bf16[4096,1536]{1,0:T(8,128)(2,1)}) %all-gather.13.cloned.1.call-update) | async-done | bytes 12582928 | tf_op jit(solution)/shard_map/all_gather | solution.py:44
  2140.4 21.8 convolution_convert_fusion
  2165.4 23.9 all-gather.17.cloned.1.call-done
  2225.4 127.7 %all-reduce.4.cloned.1.call-done = (bf16[512,1028]{0,1:T(8,128)(2,1)}, bf16[512,3072]{1,0:T(8,128)(2,1)}, bf16[512,512]{1,0:T(8,128)(2,1)}, bf16[1536,512]{1,0:T(8,128)(2,1)}) async-done(((bf16[512,1028]{0,1:T(8,128)(2,1)}, bf16[512,3072]{1,0:T(8,128)(2,1)}, bf16[512,512]{1,0:T(8,128)(2,1)}, bf16[1536,512]{1,0:T(8,128)(2,1)}), (bf16[512,1028]{0,1:T(8,128)(2,1)}, bf16[512,3072]{1,0:T(8,128)(2,1)}, ...) | async-done | bytes 6295568 | tf_op jit(solution)/shard_map/psum | solution.py:315
  2369.5 131.0 %reduce-scatter.29.cloned.1.call-done = f32[1024,512]{1,0:T(8,128)} async-done(((f32[4096,512]{1,0:T(8,128)}), f32[1024,512]{1,0:T(8,128)}) %reduce-scatter.29.cloned.1.call-update) | async-done | bytes 2097168 | tf_op jit(solution)/shard_map/reduce_scatter | solution.py:53
  2503.1 45.9 %all-reduce = (f32[2048]{0:T(1024)}, f32[128]{0:T(128)}, f32[128]{0:T(128)}, f32[2048]{0:T(1024)}) all-reduce(f32[2048]{0:T(1024)S(1)} %dynamic_update_slice.17, f32[128]{0:T(128)S(1)} %bitcast_reduce_fusion.1, f32[128]{0:T(128)S(1)} %bitcast_reduce_fusion.2, ...), channel_id=1, replica_groups=mesh['dp'=2,'wide'=4,'narrow'=4] {'dp','wide','narrow'}, use_global_device_ids=true, to_apply=%region_34.35 | all-reduce | flops 4352 | bytes 34816 | tf_op jit(solution)/shard_map/psum | solution.py:326
  2555.3 93.6 %reduce-scatter.17.cloned.1.call-done = f32[1024,512]{1,0:T(8,128)} async-done(((f32[4096,512]{1,0:T(8,128)}), f32[1024,512]{1,0:T(8,128)}) %reduce-scatter.17.cloned.1.call-update) | async-done | bytes 2097168 | tf_op jit(solution)/shard_map/reduce_scatter | solution.py:53
  (332 shorter events, 443.8 us)
Async XLA Ops:
  7.2 661.2 %copy-start = (bf16[1536,512]{1,0:T(8,128)(2,1)S(1)}, bf16[1536,512]{1,0:T(8,128)(2,1)}, u32[]{:S(2)}) copy-start(bf16[1536,512]{1,0:T(8,128)(2,1)} %param.32) | copy-start | bytes 4718596
  22.4 97.2 %all-to-all-start = ((bf16[4,1024,512]{2,1,0:T(8,128)(2,1)}), bf16[4,1024,512]{2,1,0:T(8,128)(2,1)}, u32[]{:S(2)}, u32[]{:S(2)}) async-start(bf16[4,1024,512]{2,1,0:T(8,128)(2,1)} %stack.8), calls=%async_computation | async-start | bytes 8388608 | tf_op jit(solution)/shard_map/all_to_all | solution.py:29
  27.4 230.0 %reduce-scatter.11.cloned.1.call-start = ((), (), s32[]{:S(2)}) async-start(), calls=%async_computation.14 | async-start | bytes 21135360 | tf_op jit(solution)/shard_map/reduce_scatter | solution.py:39
  132.2 126.6 %copy-start.57 = (f32[128]{0:T(128)S(1)}, f32[128]{0:T(128)}, u32[]{:S(2)}) copy-start(f32[128]{0:T(128)} %param.27) | copy-start | bytes 1540
  132.2 154.0 %all-gather.7.cloned.1.call-start = ((), (), s32[]{:S(2)}) async-start(), calls=%async_computation.15 | async-start | bytes 2621440 | tf_op jit(solution)/shard_map/all_gather | solution.py:183
  134.2 129.9 %copy-start.27 = (f32[1024,64]{0,1:T(8,128)}, f32[1024,64]{0,1:T(8,128)S(1)}, u32[]{:S(2)}) copy-start(f32[1024,64]{0,1:T(8,128)S(1)} %get-tuple-element.435) | copy-start | bytes 786436
  134.2 130.1 %copy-start.29 = (f32[1024,64]{0,1:T(8,128)}, f32[1024,64]{0,1:T(8,128)S(1)}, u32[]{:S(2)}) copy-start(f32[1024,64]{0,1:T(8,128)S(1)} %get-tuple-element.436) | copy-start | bytes 786436
  261.2 47.5 %all-gather.9.cloned.1.call-start = ((), (), s32[]{:S(2)}) async-start(), calls=%async_computation.16 | async-start | bytes 2621440 | tf_op jit(solution)/shard_map/all_gather | solution.py:184
  263.5 185.7 %all-gather.11.cloned.1.call-start = ((), (), s32[]{:S(2)}) async-start(), calls=%async_computation.17 | async-start | bytes 5242880 | tf_op jit(solution)/shard_map/all_gather | solution.py:44
  414.6 270.8 %reduce-scatter.13.cloned.1.call-start = ((), (), s32[]{:S(2)}) async-start(), calls=%async_computation.18 | async-start | bytes 10485760 | tf_op jit(solution)/shard_map/reduce_scatter | solution.py:53
  457.1 417.4 %reduce-scatter.19.cloned.1.call-start = ((), (), s32[]{:S(2)}) async-start(), calls=%async_computation.22 | async-start | bytes 31457280 | tf_op jit(solution)/shard_map/reduce_scatter | solution.py:39
  681.3 885.7 %copy-start.47 = (f32[512]{0:T(512)}, f32[512]{0:T(512)S(1)}, u32[]{:S(2)}) copy-start(f32[512]{0:T(512)S(1)} %dynamic_slice.46) | copy-start | bytes 6148
  694.6 872.5 %copy-start.43 = (f32[1024]{0:T(1024)}, f32[1024]{0:T(1024)S(1)}, u32[]{:S(2)}) copy-start(f32[1024]{0:T(1024)S(1)} %add_rsqrt_fusion.2) | copy-start | bytes 12292
  699.2 103.3 %all-to-all-start.1 = ((bf16[4,1024,512]{2,1,0:T(8,128)(2,1)}), bf16[4,1024,512]{2,1,0:T(8,128)(2,1)}, u32[]{:S(2)}, u32[]{:S(2)}) async-start(bf16[4,1024,512]{2,1,0:T(8,128)(2,1)} %stack.9), calls=%async_computation.3 | async-start | bytes 8388608 | tf_op jit(solution)/shard_map/all_to_all | solution.py:29
  709.3 514.2 %reduce-scatter.15.cloned.1.call-start = ((), (), s32[]{:S(2)}) async-start(), calls=%async_computation.19 | async-start | bytes 62914560 | tf_op jit(solution)/shard_map/reduce_scatter | solution.py:39
  828.6 563.1 %all-gather.15.cloned.1.call-start = ((), (), s32[]{:S(2)}) async-start(), calls=%async_computation.23 | async-start | bytes 31457280 | tf_op jit(solution)/shard_map/all_gather | solution.py:44
  1236.8 320.7 %reduce-scatter.21.cloned.1.call-start = ((), (), s32[]{:S(2)}) async-start(), calls=%async_computation.24 | async-start | bytes 10485760 | tf_op jit(solution)/shard_map/reduce_scatter | solution.py:53
  1412.7 154.9 %copy-start.14 = (bf16[1024,512]{1,0:T(8,128)(2,1)S(1)}, bf16[1024,512]{1,0:T(8,128)(2,1)}, u32[]{:S(2)}) copy-start(bf16[1024,512]{1,0:T(8,128)(2,1)} %param.33) | copy-start | bytes 3145732
  1412.7 333.2 %reduce-scatter.23.cloned.1.call-start = ((), (), s32[]{:S(2)}) async-start(), calls=%async_computation.25 | async-start | bytes 10485760 | tf_op jit(solution)/shard_map/reduce_scatter | solution.py:39
  1675.4 335.4 %reduce-scatter.25.cloned.1.call-start = ((), (), s32[]{:S(2)}) async-start(), calls=%async_computation.26 | async-start | bytes 2621440 | tf_op jit(solution)/shard_map/reduce_scatter | solution.py:286
  1979.5 64.9 %reduce-scatter.27.cloned.1.call-start = ((), (), s32[]{:S(2)}) async-start(), calls=%async_computation.27 | async-start | bytes 2621440 | tf_op jit(solution)/shard_map/reduce_scatter | solution.py:289
  1983.4 145.2 %all-gather.13.cloned.1.call-start = ((), (), s32[]{:S(2)}) async-start(), calls=%async_computation.20 | async-start | bytes 15728640 | tf_op jit(solution)/shard_map/all_gather | solution.py:44
  1984.2 205.1 %all-gather.17.cloned.1.call-start = ((), (), s32[]{:S(2)}) async-start(), calls=%async_computation.28 | async-start | bytes 10567680 | tf_op jit(solution)/shard_map/all_gather | solution.py:44
  2047.0 306.2 %all-reduce.4.cloned.1.call-start = ((), (), s32[]{:S(2)}) async-start(), calls=%async_computation.30 | async-start | bytes 12599296 | tf_op jit(solution)/shard_map/psum | solution.py:315
  2199.5 301.0 %reduce-scatter.29.cloned.1.call-start = ((), (), s32[]{:S(2)}) async-start(), calls=%async_computation.29 | async-start | bytes 10485760 | tf_op jit(solution)/shard_map/reduce_scatter | solution.py:53
  2212.8 436.1 %reduce-scatter.17.cloned.1.call-start = ((), (), s32[]{:S(2)}) async-start(), calls=%async_computation.21 | async-start | bytes 10485760 | tf_op jit(solution)/shard_map/reduce_scatter | solution.py:53
  2365.9 134.6 %copy-start.7 = (bf16[1024,512]{1,0:T(8,128)(2,1)S(1)}, bf16[1024,512]{1,0:T(8,128)(2,1)}, u32[]{:S(2)}) copy-start(bf16[1024,512]{1,0:T(8,128)(2,1)} %param.19) | copy-start | bytes 3145732
  2365.9 134.6 %copy-start.46 = (f32[1024]{0:T(1024)S(1)}, f32[1024]{0:T(1024)}, u32[]{:S(2)}) copy-start(f32[1024]{0:T(1024)} %copy-done.45) | copy-start | bytes 12292
  2365.9 134.7 %copy-start.52 = (f32[512]{0:T(512)S(1)}, f32[512]{0:T(512)}, u32[]{:S(2)}) copy-start(f32[512]{0:T(512)} %copy-done.51) | copy-start | bytes 6148
  2369.5 279.4 %copy-start.44 = (f32[1024]{0:T(1024)S(1)}, f32[1024]{0:T(1024)}, u32[]{:S(2)}) copy-start(f32[1024]{0:T(1024)} %copy-done.43) | copy-start | bytes 12292
  2369.5 279.4 %copy-start.48 = (f32[512]{0:T(512)S(1)}, f32[512]{0:T(512)}, u32[]{:S(2)}) copy-start(f32[512]{0:T(512)} %copy-done.47) | copy-start | bytes 6148
  2369.5 279.4 %copy-start.50 = (f32[1024]{0:T(1024)S(1)}, f32[1024]{0:T(1024)}, u32[]{:S(2)}) copy-start(f32[1024]{0:T(1024)} %copy-done.49) | copy-start | bytes 12292
  (60 other events, 782.6 us)
Sparse Core Ops, SparseCore 0:
  132.3 125.0 reduce-scatter.10
  261.3 22.5 all-gather.6
  286.0 22.5 all-gather.8
  414.7 34.4 all-gather.10
  457.2 228.1 reduce-scatter.12
  687.9 186.5 reduce-scatter.18
  877.0 346.4 reduce-scatter.14
  1236.9 154.7 all-gather.14
  1412.9 144.6 reduce-scatter.20
  1675.6 70.3 reduce-scatter.22
  1979.6 31.1 reduce-scatter.24
  2013.2 31.1 reduce-scatter.26
  2046.5 82.0 all-gather.12
  2130.6 58.6 all-gather.16
  2199.6 153.4 all-reduce.3
  2355.4 145.1 reduce-scatter.28
  2502.7 146.1 reduce-scatter.16
